TPU v7x, 32 devices: a whole 2x2x4 slice. The times are simulated.
32 devices in a mesh: rep: 2 (over y), seq: 4 (over x, core), head: 4 (over z).
Axes of the slice: x: 2, y: 2, z: 4, core: 2. Of those that a mesh axis runs over, the one named last changes fastest.
Arguments:
- query: bfloat16 [32768, 2048], P(('rep', 'seq', 'head')), parts along dimension 0, may hold values from -6 to 6
- key: bfloat16 [32768, 2048], P(('rep', 'seq', 'head')), parts along dimension 0, may hold values from -6 to 6
- value: bfloat16 [32768, 2048], P(('rep', 'seq', 'head')), parts along dimension 0, may hold values from -6 to 6
- grad_out: bfloat16 [32768, 2048], P(('rep', 'seq', 'head')), parts along dimension 0, may hold values from -6 to 6
- level_weights: bfloat16 [32768, 128], P(('rep', 'seq', 'head')), parts along dimension 0, may hold values from 0.25 to 4
Outputs:
- attended: bfloat16 [32768, 2048], P(('rep', 'seq', 'head')), parts along dimension 0
- grad_query: bfloat16 [32768, 2048], P(('rep', 'seq', 'head')), parts along dimension 0
- grad_key: bfloat16 [32768, 2048], P(('rep', 'seq', 'head')), parts along dimension 0
- grad_value: bfloat16 [32768, 2048], P(('rep', 'seq', 'head')), parts along dimension 0
- grad_weights: bfloat16 [32768, 128], P(('rep', 'seq', 'head')), parts along dimension 0
There are 2 independent parts, one for each index of `rep`. A program takes and returns all parts, laid end to end along the dimension named above; each array names one. Nothing has to cross between parts.
All inputs are finite; a program needn't handle non-finite values.
Results may differ from a plain program's by a relative error of at most 0.0056.
Values may be sent and summed in bfloat16 or wider, within the bound.
A program may use at most 384 MiB of HBM per device.

v0:
```python
import math
import jax
import jax.numpy as jnp
from jax import lax
from jax.sharding import PartitionSpec as P

DH = 128
C = 128
LEVELS = 8


def level_scale(level):
    if level == 0:
        return 1.0 / math.sqrt(DH * C)
    return 1.0 / math.sqrt(DH * C * 2 ** (level - 1))


def bucket_matrix(count, level_bit):
    rows = jnp.arange(count, dtype=jnp.int32)[:, None]
    columns = jnp.arange(count, dtype=jnp.int32)[None, :]
    stride = 2**level_bit
    reading = rows // stride % 2 == 1
    inside = columns // stride == rows // (2 * stride) * 2
    return jnp.where(reading & inside, 1.0, 0.0).astype(jnp.float32)


def local_part(query, key, value, grad_out, level_weights):
    heads = query.shape[1] // DH
    stretches = query.shape[0] // C
    blocks = (stretches, C, heads, DH)
    query_blocks = query.reshape(blocks)
    key_blocks = key.reshape(blocks)
    value_blocks = value.reshape(blocks)
    grad_blocks = grad_out.reshape(blocks)
    weights = level_weights.reshape(stretches, C, heads, LEVELS).astype(jnp.float32)
    mask = jnp.tril(jnp.ones((C, C), jnp.float32))
    scores = jnp.einsum(
        "ntgd,nsgd->ngts", query_blocks, key_blocks, preferred_element_type=jnp.float32
    ) * (level_scale(0) * mask)
    first = jnp.transpose(weights[..., 0], (0, 2, 1))[..., None]
    probs = (first * scores).astype(jnp.bfloat16)
    attended = jnp.einsum(
        "ngts,nsgd->ntgd", probs, value_blocks, preferred_element_type=jnp.float32
    )
    grad_probs = jnp.einsum(
        "ntge,nsge->ngts", grad_blocks, value_blocks, preferred_element_type=jnp.float32
    )
    grad_levels = [jnp.transpose(jnp.sum(scores * grad_probs, axis=-1), (0, 2, 1))]
    grad_scores = (first * grad_probs * (level_scale(0) * mask)).astype(jnp.bfloat16)
    grad_query = jnp.einsum(
        "ngts,nsgd->ntgd", grad_scores, key_blocks, preferred_element_type=jnp.float32
    )
    grad_key = jnp.einsum(
        "ngts,ntgd->nsgd", grad_scores, query_blocks, preferred_element_type=jnp.float32
    )
    grad_value = jnp.einsum(
        "ngts,ntge->nsge", probs, grad_blocks, preferred_element_type=jnp.float32
    )
    states = jnp.einsum(
        "nsgd,nsge->ngde", key_blocks, value_blocks, preferred_element_type=jnp.float32
    )
    products = []
    for level in range(1, LEVELS):
        weighted = (weights[..., level : level + 1] * query_blocks).astype(jnp.bfloat16)
        products.append(
            jnp.einsum("ntgd,ntge->ngde", weighted, grad_blocks, preferred_element_type=jnp.float32)
        )
    blocks_all = (query_blocks, key_blocks, value_blocks, grad_blocks, weights)
    partial_value = (attended, grad_levels, grad_query, grad_key, grad_value)
    return (blocks_all, partial_value, states, products)


def finish(blocks_all, partial_value, states, products, cross_reads, cross_adjoint):
    query_blocks, key_blocks, value_blocks, grad_blocks, weights = blocks_all
    attended, grad_levels, grad_query, grad_key, grad_value = partial_value
    stretches = query_blocks.shape[0]
    heads = query_blocks.shape[2]
    local_bits = stretches.bit_length() - 1
    adjoint = jnp.zeros((stretches, heads, DH, DH), jnp.float32)
    for level in range(1, LEVELS):
        factor = level_scale(level)
        if level <= local_bits:
            mapping = bucket_matrix(stretches, level - 1)
            summed = jnp.einsum("ij,jgde->igde", mapping, states, precision=lax.Precision.HIGHEST)
            read_state = (factor * summed).astype(jnp.bfloat16)
            reads = jnp.einsum(
                "ntgd,ngde->ntge", query_blocks, read_state, preferred_element_type=jnp.float32
            )
            backward = jnp.einsum(
                "ntge,ngde->ntgd", grad_blocks, read_state, preferred_element_type=jnp.float32
            )
            adjoint = adjoint + factor * jnp.einsum(
                "ij,igde->jgde", mapping, products[level - 1], precision=lax.Precision.HIGHEST
            )
        else:
            index = level - 1 - local_bits
            read_state = (factor * cross_reads[index]).astype(jnp.bfloat16)
            reads = jnp.einsum(
                "ntgd,gde->ntge", query_blocks, read_state, preferred_element_type=jnp.float32
            )
            backward = jnp.einsum(
                "ntge,gde->ntgd", grad_blocks, read_state, preferred_element_type=jnp.float32
            )
            adjoint = adjoint + factor * cross_adjoint[index][None]
        weight = weights[..., level : level + 1]
        attended = attended + weight * reads
        grad_levels.append(jnp.sum(grad_blocks.astype(jnp.float32) * reads, axis=-1))
        grad_query = grad_query + weight * backward
    adjoint_low = adjoint.astype(jnp.bfloat16)
    grad_key = grad_key + jnp.einsum(
        "nsge,ngde->nsgd", value_blocks, adjoint_low, preferred_element_type=jnp.float32
    )
    grad_value = grad_value + jnp.einsum(
        "nsgd,ngde->nsge", key_blocks, adjoint_low, preferred_element_type=jnp.float32
    )

    def flatten(array, width):
        return array.reshape(stretches * C, heads * width).astype(jnp.bfloat16)

    return (
        flatten(attended, DH),
        flatten(grad_query, DH),
        flatten(grad_key, DH),
        flatten(grad_value, DH),
        flatten(jnp.stack(grad_levels, axis=-1), LEVELS),
    )


def cross_inputs(states, products, stretches, cross_bits):
    local_bits = stretches.bit_length() - 1
    cross_total = jnp.sum(states, axis=0)
    cross_products = jnp.stack(
        [jnp.sum(products[local_bits + level_bit], axis=0) for level_bit in range(cross_bits)]
    )
    return (cross_total, cross_products)


def shards(query, key, value, grad_out, level_weights):
    query, key, value, grad_out, level_weights = (
        lax.all_to_all(query, "head", split_axis=1, concat_axis=0, tiled=True),
        lax.all_to_all(key, "head", split_axis=1, concat_axis=0, tiled=True),
        lax.all_to_all(value, "head", split_axis=1, concat_axis=0, tiled=True),
        lax.all_to_all(grad_out, "head", split_axis=1, concat_axis=0, tiled=True),
        lax.all_to_all(level_weights, "head", split_axis=1, concat_axis=0, tiled=True),
    )
    blocks_all, partial_value, states, products = local_part(
        query, key, value, grad_out, level_weights
    )
    stretches = states.shape[0]
    cross_bits = lax.axis_size("seq").bit_length() - 1
    position = lax.axis_index("seq")
    cross_total, cross_products = cross_inputs(states, products, stretches, cross_bits)
    totals = lax.all_gather(cross_total[None], "seq", axis=0, tiled=True)
    sums = lax.all_gather(cross_products[None], "seq", axis=0, tiled=True)
    count = totals.shape[0]
    source = jnp.arange(count, dtype=jnp.int32)[:, None]
    powers = (2 ** jnp.arange(cross_bits, dtype=jnp.int32))[None, :]
    base = position // (2 * powers) * (2 * powers)
    owned = position // powers % 2
    lower = (source >= base) & (source < base + powers)
    upper = (source >= base + powers) & (source < base + 2 * powers)
    forward = jnp.where(lower & (owned == 1), 1.0, 0.0).astype(jnp.float32)
    backward = jnp.where(upper & (owned == 0), 1.0, 0.0).astype(jnp.float32)
    read_sum = jnp.einsum("qb,qgde->bgde", forward, totals, precision=lax.Precision.HIGHEST)
    adjoint_sum = jnp.einsum("qb,qbgde->bgde", backward, sums, precision=lax.Precision.HIGHEST)
    results = finish(blocks_all, partial_value, states, products, read_sum, adjoint_sum)
    return (
        lax.all_to_all(results[0], "head", split_axis=0, concat_axis=1, tiled=True),
        lax.all_to_all(results[1], "head", split_axis=0, concat_axis=1, tiled=True),
        lax.all_to_all(results[2], "head", split_axis=0, concat_axis=1, tiled=True),
        lax.all_to_all(results[3], "head", split_axis=0, concat_axis=1, tiled=True),
        lax.all_to_all(results[4], "head", split_axis=0, concat_axis=1, tiled=True),
    )


def solution(mesh):
    return jax.shard_map(
        shards,
        mesh=mesh,
        in_specs=(
            P(("rep", "seq", "head"), None),
            P(("rep", "seq", "head"), None),
            P(("rep", "seq", "head"), None),
            P(("rep", "seq", "head"), None),
            P(("rep", "seq", "head"), None),
        ),
        out_specs=(
            P(("rep", "seq", "head"), None),
            P(("rep", "seq", "head"), None),
            P(("rep", "seq", "head"), None),
            P(("rep", "seq", "head"), None),
            P(("rep", "seq", "head"), None),
        ),
        check_vma=False,
    )
```

profile of v0, /device:TPU:0, one launch (start us, length us, event | category | flops | bytes accessed | tf_op | source)
XLA Modules:
  0.0 1145.0 jit_solution(13611935831016947654)
XLA Ops:
  33.7 87.2 %all-to-all-done.5 = bf16[1024,4,512]{2,0,1:T(8,128)(2,1)} async-done(((bf16[1024,4,512]{2,0,1:T(8,128)(2,1)}), bf16[1024,4,512]{2,0,1:T(8,128)(2,1)}, u32[]{:S(2)}, u32[]{:S(2)}) %all-to-all-start.5) | async-done | bytes 4194336 | tf_op jit(solution)/shard_map/all_to_all | solution.py:143
  130.3 88.1 %all-to-all-done.3 = bf16[1024,4,512]{2,0,1:T(8,128)(2,1)} async-done(((bf16[1024,4,512]{2,0,1:T(8,128)(2,1)}), bf16[1024,4,512]{2,0,1:T(8,128)(2,1)}, u32[]{:S(2)}, u32[]{:S(2)}) %all-to-all-start.3) | async-done | bytes 4194336 | tf_op jit(solution)/shard_map/all_to_all | solution.py:142
  227.9 88.1 %all-to-all-done.2 = bf16[1024,4,512]{2,0,1:T(8,128)(2,1)} async-done(((bf16[1024,4,512]{2,0,1:T(8,128)(2,1)}), bf16[1024,4,512]{2,0,1:T(8,128)(2,1)}, u32[]{:S(2)}, u32[]{:S(2)}) %all-to-all-start.2) | async-done | bytes 4194336 | tf_op jit(solution)/shard_map/all_to_all | solution.py:141
  323.9 6.9 reshape.630
  330.8 6.9 reshape.629
  337.7 6.9 reshape.628
  344.6 69.0 %all-to-all-done.1 = bf16[1024,4,512]{2,0,1:T(8,128)(2,1)} async-done(((bf16[1024,4,512]{2,0,1:T(8,128)(2,1)}), bf16[1024,4,512]{2,0,1:T(8,128)(2,1)}, u32[]{:S(2)}, u32[]{:S(2)}) %all-to-all-start.1) | async-done | bytes 4194336 | tf_op jit(solution)/shard_map/all_to_all | solution.py:140
  413.6 6.9 reshape.627
  433.1 11.7 %multiply_convert_fusion.1 = bf16[32,4,128,128]{3,0,2,1:T(8,128)(2,1)S(1)} fusion(f32[32,4,128,128]{3,2,1,0:T(8,128)S(1)} %get-tuple-element.42, s32[32]{0:T(128)S(1)} %get-tuple-element.47, s32[32]{0:T(128)S(1)} %get-tuple-element.46, pred[32]{0:T(512)(128)(4,1)S(1)} %fusion.227), kind=kOutput, calls=%fused_computation.75 | convolution fusion | flops 809503744 | bytes 12583200 | tf_op jit(solution)/shard_map/ij,jgde->igde/dot_general | solution.py:84
  444.8 7.9 fusion.73
  452.7 11.9 %multiply_convert_fusion.2 = bf16[32,4,128,128]{3,0,2,1:T(8,128)(2,1)S(1)} fusion(f32[32,4,128,128]{3,2,1,0:T(8,128)S(1)} %get-tuple-element.42, s32[32]{0:T(128)S(1)} %get-tuple-element.49, s32[32]{0:T(128)S(1)} %get-tuple-element.48, pred[32]{0:T(512)(128)(4,1)S(1)} %fusion.226), kind=kOutput, calls=%fused_computation.76 | convolution fusion | flops 809503744 | bytes 12583200 | tf_op jit(solution)/shard_map/ij,jgde->igde/dot_general | solution.py:84
  466.6 7.9 fusion.77
  474.5 10.5 fusion.75
  485.0 10.9 fusion.79
  496.0 11.7 %multiply_convert_fusion.3 = bf16[32,4,128,128]{3,0,2,1:T(8,128)(2,1)S(1)} fusion(f32[32,4,128,128]{3,2,1,0:T(8,128)S(1)} %get-tuple-element.42, s32[32]{0:T(128)S(1)} %get-tuple-element.51, s32[32]{0:T(128)S(1)} %get-tuple-element.50, pred[32]{0:T(512)(128)(4,1)S(1)} %fusion.225), kind=kOutput, calls=%fused_computation.77 | convolution fusion | flops 809503744 | bytes 12583200 | tf_op jit(solution)/shard_map/ij,jgde->igde/dot_general | solution.py:84
  509.8 7.8 fusion.81
  517.6 10.6 fusion.83
  528.2 11.7 %multiply_convert_fusion.5 = bf16[32,4,128,128]{3,0,2,1:T(8,128)(2,1)S(1)} fusion(f32[32,4,128,128]{3,2,1,0:T(8,128)S(1)} %get-tuple-element.42, s32[32]{0:T(128)S(1)} %broadcast_multiply_fusion.3, pred[32]{0:T(512)(128)(4,1)S(1)} %fusion.223), kind=kOutput, calls=%fused_computation.79 | convolution fusion | flops 809503744 | bytes 12583072 | tf_op jit(solution)/shard_map/ij,jgde->igde/dot_general | solution.py:84
  539.9 7.9 fusion.89
  547.9 15.7 %multiply_convert_fusion.4 = bf16[32,4,128,128]{3,0,2,1:T(8,128)(2,1)S(1)} fusion(f32[32,4,128,128]{3,2,1,0:T(8,128)} %copy-done.9, s32[32]{0:T(128)S(1)} %get-tuple-element.53, s32[32]{0:T(128)S(1)} %get-tuple-element.52, pred[32]{0:T(512)(128)(4,1)S(1)} %fusion.224), kind=kOutput, calls=%fused_computation.78 | convolution fusion | flops 809503744 | bytes 12583200 | tf_op jit(solution)/shard_map/ij,jgde->igde/dot_general | solution.py:84
  563.7 8.0 fusion.85
  571.7 7.3 fusion.56
  579.0 13.1 %fusion.32 = f32[32,4,128,128]{3,0,2,1:T(8,128)} fusion(f32[32,4,128,128]{3,2,1,0:T(8,128)S(1)} %fusion.56, s32[32]{0:T(128)S(1)} %get-tuple-element.47, s32[32]{0:T(128)S(1)} %get-tuple-element.46, pred[32]{0:T(512)(128)(4,1)S(1)} %fusion.227), kind=kOutput, calls=%fused_computation.62 | convolution fusion | flops 805309440 | bytes 16777504 | tf_op jit(solution)/shard_map/ij,igde->jgde/dot_general | solution.py:92
  598.8 11.1 multiply_reduce_fusion
  627.5 6.9 fusion.139
  634.4 25.6 %fusion.13 = (bf16[32,128,4]{1,2,0:T(4,128)(2,1)S(1)}, bf16[32,128,4]{1,2,0:T(4,128)(2,1)}, bf16[32,128,4]{1,2,0:T(4,128)(2,1)S(1)}, bf16[32,128,4]{1,2,0:T(4,12...) fusion(bf16[32,128,4,128]{3,2,1,0:T(4,128)(2,1)S(1)} %copy-done, ...), kind=kOutput, calls=%fused_computation.27 | convolution fusion | flops 568213504 | bytes 67469312 | tf_op jit(solution)/shard_map/ntgd,gde->ntge/dot_general | solution.py:98
  673.7 26.1 %fusion.25 = bf16[32,128,4,128]{3,1,2,0:T(8,128)(2,1)S(1)} fusion(f32[4,128,32,128]{1,3,0,2:T(8,128)} %get-tuple-element.45, f32[4,128,32,128]{1,3,0,2:T(8,128)} %fusion.139, f32[32,4,128,128]{2,3,1,0:T(8,128)} %fusion.73, f32[32,4,128,128]{2,3,1,0:T(8,128)} %fusion.77, f32[32,4,128,128]{2,3,1,0:T(8,128)} %fusion.81, f32[32,4,128,128]{2,3,1,0:T(8,128)} %fusion.85, ...), kind=kOutput, calls=%fused_computation.49 | convolution fusion | flops 574619648 | bytes 76087296 | tf_op jit(solution)/shard_map/ngts,nsgd->ntgd/dot_general | solution.py:42
  705.7 7.2 convert_element_type.131
  718.8 11.9 %fusion.87 = f32[32,4,128,128]{2,3,1,0:T(8,128)} fusion(bf16[32,4,128,128]{3,0,2,1:T(8,128)(2,1)} %copy-done.15, bf16[32,128,4,128]{3,2,1,0:T(4,128)(2,1)} %reshape.630), kind=kOutput, calls=%fused_computation.123 | convolution fusion | flops 536870912 | bytes 16777216 | tf_op jit(solution)/shard_map/ntge,ngde->ntgd/dot_general | solution.py:89
  731.6 17.4 %fusion.34 = f32[32,4,128,128]{3,0,2,1:T(8,128)} fusion(f32[32,4,128,128]{3,2,1,0:T(8,128)} %fusion.58, s32[32]{0:T(128)S(1)} %copy-done.42, s32[32]{0:T(128)S(1)} %copy-done.40, pred[32]{0:T(512)(128)(4,1)S(1)} %copy-done.38), kind=kOutput, calls=%fused_computation.64 | convolution fusion | flops 805309440 | bytes 16777504 | tf_op jit(solution)/shard_map/ij,igde->jgde/dot_general | solution.py:92
  755.7 8.6 fusion.105
  777.6 21.7 %fusion.17 = bf16[32,128,4,128]{3,1,2,0:T(8,128)(2,1)} fusion(f32[4,128,32,128]{1,3,0,2:T(8,128)} %fusion.133, f32[4,128,32,128]{1,3,0,2:T(8,128)} %fusion.137, f32[32,4,128,128]{2,3,1,0:T(8,128)S(1)} %bitcast.276, f32[32,4,128,128]{2,3,1,0:T(8,128)S(1)} %bitcast.278, f32[32,4,128,128]{2,3,1,0:T(8,128)} %fusion.83, f32[32,4,128,128]{2,3,1,0:T(8,128)} %fusion.87, ...), kind=kOutput, calls=%fused_computation.34 | convolution fusion | flops 568328192 | bytes 71761920 | tf_op jit(solution)/shard_map/ntge,ngde->ntgd/dot_general | solution.py:89
  799.3 8.2 copy.351
  807.5 7.2 convert_element_type.134
  819.8 17.2 %fusion.36 = f32[32,4,128,128]{3,0,2,1:T(8,128)} fusion(f32[32,4,128,128]{3,2,1,0:T(8,128)} %fusion.60, s32[32]{0:T(128)S(1)} %copy-done.36, s32[32]{0:T(128)S(1)} %copy-done.34, pred[32]{0:T(512)(128)(4,1)S(1)} %copy-done.28), kind=kOutput, calls=%fused_computation.66 | convolution fusion | flops 805309440 | bytes 16777504 | tf_op jit(solution)/shard_map/ij,igde->jgde/dot_general | solution.py:92
  837.1 7.4 fusion.62
  844.5 13.4 %fusion.38 = f32[32,4,128,128]{3,0,2,1:T(8,128)} fusion(f32[32,4,128,128]{3,2,1,0:T(8,128)S(1)} %fusion.62, s32[32]{0:T(128)S(1)} %copy-done.32, s32[32]{0:T(128)S(1)} %copy-done.30, pred[32]{0:T(512)(128)(4,1)S(1)} %copy-done.26), kind=kOutput, calls=%fused_computation.68 | convolution fusion | flops 805309440 | bytes 16777504 | tf_op jit(solution)/shard_map/ij,igde->jgde/dot_general | solution.py:92
  857.9 6.7 fusion.64
  876.9 25.1 %add_convert_fusion = bf16[32,4,128,128]{3,0,2,1:T(8,128)(2,1)} fusion(f32[32,4,128,128]{3,0,2,1:T(8,128)} %fusion.32, f32[32,4,128,128]{3,0,2,1:T(8,128)} %fusion.34, f32[32,4,128,128]{3,0,2,1:T(8,128)} %fusion.36, f32[32,4,128,128]{3,0,2,1:T(8,128)} %fusion.38, f32[4,128,128]{2,1,0:T(8,128)S(1)} %bitcast.294, f32[4,128,128]{2,1,0:T(8,128)S(1)} %bitcast.293, ...), kind=kOutput, calls=%fused_computation.73 | convolution fusion | flops 830475264 | bytes 46661792 | tf_op jit(solution)/shard_map/ij,igde->jgde/dot_general | solution.py:92
  902.0 7.7 copy.380
  909.7 7.2 fusion.15
  922.9 7.2 convert_element_type.145
  935.4 9.4 fusion.129
  944.8 9.8 fusion.14
  954.6 8.2 copy.383
  962.8 7.2 convert_element_type.147
  970.0 57.5 %all-to-all-done.7 = bf16[4,1024,512]{2,1,0:T(8,128)(2,1)} async-done(((bf16[4,1024,512]{2,1,0:T(8,128)(2,1)}), bf16[4,1024,512]{2,1,0:T(8,128)(2,1)}, u32[]{:S(2)}, u32[]{:S(2)}) %all-to-all-start.7) | async-done | bytes 4194336 | tf_op jit(solution)/shard_map/all_to_all | solution.py:170
  1071.1 54.0 %all-to-all-done.8 = bf16[4,1024,512]{2,1,0:T(8,128)(2,1)} async-done(((bf16[4,1024,512]{2,1,0:T(8,128)(2,1)}), bf16[4,1024,512]{2,1,0:T(8,128)(2,1)}, u32[]{:S(2)}, u32[]{:S(2)}) %all-to-all-start.8) | async-done | bytes 4194336 | tf_op jit(solution)/shard_map/all_to_all | solution.py:171
  (199 shorter events, 225.2 us)
Async XLA Ops:
  9.0 15.2 %all-to-all-start = ((bf16[1024,4,32]{0,2,1:T(8,128)(2,1)}), bf16[1024,4,32]{0,2,1:T(8,128)(2,1)S(1)}, u32[]{:S(2)}, u32[]{:S(2)}) async-start(bf16[1024,4,32]{0,2,1:T(8,128)(2,1)} %bitcast), calls=%async_computation | async-start | bytes 524288 | tf_op jit(solution)/shard_map/all_to_all | solution.py:144
  24.2 96.7 %all-to-all-start.5 = ((bf16[1024,4,512]{2,0,1:T(8,128)(2,1)}), bf16[1024,4,512]{2,0,1:T(8,128)(2,1)}, u32[]{:S(2)}, u32[]{:S(2)}) async-start(bf16[1024,4,512]{2,0,1:T(8,128)(2,1)} %bitcast.280), calls=%async_computation.5 | async-start | bytes 8388608 | tf_op jit(solution)/shard_map/all_to_all | solution.py:143
  120.9 97.5 %all-to-all-start.3 = ((bf16[1024,4,512]{2,0,1:T(8,128)(2,1)}), bf16[1024,4,512]{2,0,1:T(8,128)(2,1)}, u32[]{:S(2)}, u32[]{:S(2)}) async-start(bf16[1024,4,512]{2,0,1:T(8,128)(2,1)} %bitcast.281), calls=%async_computation.3 | async-start | bytes 8388608 | tf_op jit(solution)/shard_map/all_to_all | solution.py:142
  218.4 97.6 %all-to-all-start.2 = ((bf16[1024,4,512]{2,0,1:T(8,128)(2,1)}), bf16[1024,4,512]{2,0,1:T(8,128)(2,1)}, u32[]{:S(2)}, u32[]{:S(2)}) async-start(bf16[1024,4,512]{2,0,1:T(8,128)(2,1)} %bitcast.282), calls=%async_computation.2 | async-start | bytes 8388608 | tf_op jit(solution)/shard_map/all_to_all | solution.py:141
  316.0 97.6 %all-to-all-start.1 = ((bf16[1024,4,512]{2,0,1:T(8,128)(2,1)}), bf16[1024,4,512]{2,0,1:T(8,128)(2,1)}, u32[]{:S(2)}, u32[]{:S(2)}) async-start(bf16[1024,4,512]{2,0,1:T(8,128)(2,1)} %bitcast.279), calls=%async_computation.1 | async-start | bytes 8388608 | tf_op jit(solution)/shard_map/all_to_all | solution.py:140
  320.9 301.8 %all-gather.5.cloned.1.call-start = ((), (), s32[]{:S(2)}) async-start(), calls=%async_computation.10 | async-start | bytes 1310720 | tf_op jit(solution)/shard_map/all_gather | solution.py:153
  321.5 206.7 %copy-start.43 = (s32[32]{0:T(128)}, s32[32]{0:T(128)S(1)}, u32[]{:S(2)}) copy-start(s32[32]{0:T(128)S(1)} %broadcast_multiply_fusion.3) | copy-start | bytes 388
  321.5 206.7 %copy-start.45 = (pred[32]{0:T(512)(128)(4,1)}, pred[32]{0:T(512)(128)(4,1)S(1)}, u32[]{:S(2)}) copy-start(pred[32]{0:T(512)(128)(4,1)S(1)} %fusion.223) | copy-start | bytes 100
  321.6 131.1 %copy-start.37 = (pred[32]{0:T(512)(128)(4,1)}, pred[32]{0:T(512)(128)(4,1)S(1)}, u32[]{:S(2)}) copy-start(pred[32]{0:T(512)(128)(4,1)S(1)} %fusion.226) | copy-start | bytes 100
  321.6 174.4 %copy-start.27 = (pred[32]{0:T(512)(128)(4,1)}, pred[32]{0:T(512)(128)(4,1)S(1)}, u32[]{:S(2)}) copy-start(pred[32]{0:T(512)(128)(4,1)S(1)} %fusion.225) | copy-start | bytes 100
  321.6 226.3 %copy-start.25 = (pred[32]{0:T(512)(128)(4,1)}, pred[32]{0:T(512)(128)(4,1)S(1)}, u32[]{:S(2)}) copy-start(pred[32]{0:T(512)(128)(4,1)S(1)} %fusion.224) | copy-start | bytes 100
  322.1 130.6 %copy-start.39 = (s32[32]{0:T(128)}, s32[32]{0:T(128)S(1)}, u32[]{:S(2)}) copy-start(s32[32]{0:T(128)S(1)} %get-tuple-element.48) | copy-start | bytes 388
  322.1 130.6 %copy-start.41 = (s32[32]{0:T(128)}, s32[32]{0:T(128)S(1)}, u32[]{:S(2)}) copy-start(s32[32]{0:T(128)S(1)} %get-tuple-element.49) | copy-start | bytes 388
  322.1 173.9 %copy-start.33 = (s32[32]{0:T(128)}, s32[32]{0:T(128)S(1)}, u32[]{:S(2)}) copy-start(s32[32]{0:T(128)S(1)} %get-tuple-element.50) | copy-start | bytes 388
  322.1 173.9 %copy-start.35 = (s32[32]{0:T(128)}, s32[32]{0:T(128)S(1)}, u32[]{:S(2)}) copy-start(s32[32]{0:T(128)S(1)} %get-tuple-element.51) | copy-start | bytes 388
  322.1 225.7 %copy-start.29 = (s32[32]{0:T(128)}, s32[32]{0:T(128)S(1)}, u32[]{:S(2)}) copy-start(s32[32]{0:T(128)S(1)} %get-tuple-element.52) | copy-start | bytes 388
  322.1 225.7 %copy-start.31 = (s32[32]{0:T(128)}, s32[32]{0:T(128)S(1)}, u32[]{:S(2)}) copy-start(s32[32]{0:T(128)S(1)} %get-tuple-element.53) | copy-start | bytes 388
  426.8 101.4 %copy-start.9 = (f32[32,4,128,128]{3,2,1,0:T(8,128)}, f32[32,4,128,128]{3,2,1,0:T(8,128)S(1)}, u32[]{:S(2)}) copy-start(f32[32,4,128,128]{3,2,1,0:T(8,128)S(1)} %get-tuple-element.42) | copy-start | bytes 25165828
  444.8 7.9 copy-start.16
  466.6 7.9 copy-start
  539.9 7.9 copy-start.13
  547.9 15.7 %copy-start.6 = (bf16[32,128,4,128]{3,2,1,0:T(4,128)(2,1)S(1)}, bf16[32,128,4,128]{3,2,1,0:T(4,128)(2,1)}, u32[]{:S(2)}) copy-start(bf16[32,128,4,128]{3,2,1,0:T(4,128)(2,1)} %reshape.627) | copy-start | bytes 12582916
  563.6 8.0 copy-start.15
  563.6 8.0 copy-start.1
  669.9 43.0 %all-to-all-start.9 = ((bf16[4,1024,32]{1,2,0:T(8,128)(2,1)}), bf16[4,1024,32]{1,2,0:T(8,128)(2,1)S(1)}, u32[]{:S(2)}, u32[]{:S(2)}) async-start(bf16[4,1024,32]{1,2,0:T(8,128)(2,1)} %copy.387), calls=%async_computation.9 | async-start | bytes 524288 | tf_op jit(solution)/shard_map/all_to_all | solution.py:172
  713.6 101.1 %all-to-all-start.4 = ((bf16[4,1024,512]{2,1,0:T(8,128)(2,1)}), bf16[4,1024,512]{2,1,0:T(8,128)(2,1)}, u32[]{:S(2)}, u32[]{:S(2)}) async-start(bf16[4,1024,512]{2,1,0:T(8,128)(2,1)} %convert_element_type.131), calls=%async_computation.4 | async-start | bytes 8388608 | tf_op jit(solution)/shard_map/all_to_all | solution.py:168
  718.7 12.0 %copy-start.22 = (f32[1,4,128,128]{3,2,1,0:T(8,128)S(1)}, f32[1,4,128,128]{3,2,1,0:T(8,128)}, u32[]{:S(2)}) copy-start(f32[1,4,128,128]{3,2,1,0:T(8,128)} %fusion.124) | copy-start | bytes 786436
  718.7 12.0 %copy-start.23 = (f32[1,4,128,128]{3,2,1,0:T(8,128)S(1)}, f32[1,4,128,128]{3,2,1,0:T(8,128)}, u32[]{:S(2)}) copy-start(f32[1,4,128,128]{3,2,1,0:T(8,128)} %fusion.121) | copy-start | bytes 786436
  718.7 12.8 %copy-start.38 = (pred[32]{0:T(512)(128)(4,1)S(1)}, pred[32]{0:T(512)(128)(4,1)}, u32[]{:S(2)}) copy-start(pred[32]{0:T(512)(128)(4,1)} %copy-done.37) | copy-start | bytes 100
  718.7 12.8 %copy-start.40 = (s32[32]{0:T(128)S(1)}, s32[32]{0:T(128)}, u32[]{:S(2)}) copy-start(s32[32]{0:T(128)} %copy-done.39) | copy-start | bytes 388
  718.7 12.8 %copy-start.42 = (s32[32]{0:T(128)S(1)}, s32[32]{0:T(128)}, u32[]{:S(2)}) copy-start(s32[32]{0:T(128)} %copy-done.41) | copy-start | bytes 388
  718.7 150.7 %all-gather.7.cloned.1.call-start = ((), (), s32[]{:S(2)}) async-start(), calls=%async_computation.11 | async-start | bytes 2621440 | tf_op jit(solution)/shard_map/all_gather | solution.py:154
  731.5 17.5 %copy-start.3 = (bf16[32,128,4,128]{3,2,1,0:T(4,128)(2,1)S(1)}, bf16[32,128,4,128]{3,2,1,0:T(4,128)(2,1)}, u32[]{:S(2)}) copy-start(bf16[32,128,4,128]{3,2,1,0:T(4,128)(2,1)} %reshape.630) | copy-start | bytes 12582916
  731.6 17.5 %copy-start.7 = (bf16[32,128,4,128]{3,2,1,0:T(4,128)(2,1)S(1)}, bf16[32,128,4,128]{3,2,1,0:T(4,128)(2,1)}, u32[]{:S(2)}) copy-start(bf16[32,128,4,128]{3,2,1,0:T(4,128)(2,1)} %reshape.627) | copy-start | bytes 12582916
  755.7 8.6 copy-start.19
  764.3 11.0 slice-start.2
  764.3 11.0 slice-start.4
  769.8 7.8 copy-start.14
  814.7 115.3 %all-to-all-start.6 = ((bf16[4,1024,512]{2,1,0:T(8,128)(2,1)}), bf16[4,1024,512]{2,1,0:T(8,128)(2,1)}, u32[]{:S(2)}, u32[]{:S(2)}) async-start(bf16[4,1024,512]{2,1,0:T(8,128)(2,1)} %convert_element_type.134), calls=%async_computation.6 | async-start | bytes 8388608 | tf_op jit(solution)/shard_map/all_to_all | solution.py:169
  819.8 17.3 %copy-start.4 = (bf16[32,128,4,128]{3,2,1,0:T(4,128)(2,1)S(1)}, bf16[32,128,4,128]{3,2,1,0:T(4,128)(2,1)}, u32[]{:S(2)}) copy-start(bf16[32,128,4,128]{3,2,1,0:T(4,128)(2,1)} %reshape.630) | copy-start | bytes 12582916
  819.8 17.3 %copy-start.8 = (bf16[32,128,4,128]{3,2,1,0:T(4,128)(2,1)S(1)}, bf16[32,128,4,128]{3,2,1,0:T(4,128)(2,1)}, u32[]{:S(2)}) copy-start(bf16[32,128,4,128]{3,2,1,0:T(4,128)(2,1)} %reshape.627) | copy-start | bytes 12582916
  844.5 20.2 %slice-start = ((s8[8388608]{0:T(1024)(128)(4,1)}), s8[4194304]{0:T(1024)(128)(4,1)S(1)}, s32[]{:S(2)}) async-start(s8[8388608]{0:T(1024)(128)(4,1)} %bitcast.273), calls=%async_computation.12 | async-start | bytes 8388608
  869.4 7.5 copy-start.44
  869.4 7.5 copy-start.46
  930.0 97.5 %all-to-all-start.7 = ((bf16[4,1024,512]{2,1,0:T(8,128)(2,1)}), bf16[4,1024,512]{2,1,0:T(8,128)(2,1)}, u32[]{:S(2)}, u32[]{:S(2)}) async-start(bf16[4,1024,512]{2,1,0:T(8,128)(2,1)} %convert_element_type.145), calls=%async_computation.7 | async-start | bytes 8388608 | tf_op jit(solution)/shard_map/all_to_all | solution.py:170
  935.4 9.4 copy-start.12
  970.0 62.4 %copy-start.21 = (bf16[4,1024,32]{1,2,0:T(8,128)(2,1)S(1)}, bf16[4,1024,32]{1,2,0:T(8,128)(2,1)}, u32[]{:S(2)}) copy-start(bf16[4,1024,32]{1,2,0:T(8,128)(2,1)} %copy-done.20) | copy-start | bytes 786436
  1027.5 97.6 %all-to-all-start.8 = ((bf16[4,1024,512]{2,1,0:T(8,128)(2,1)}), bf16[4,1024,512]{2,1,0:T(8,128)(2,1)}, u32[]{:S(2)}, u32[]{:S(2)}) async-start(bf16[4,1024,512]{2,1,0:T(8,128)(2,1)} %convert_element_type.147), calls=%async_computation.8 | async-start | bytes 8388608 | tf_op jit(solution)/shard_map/all_to_all | solution.py:171
  (17 other events, 91.8 us)
Sparse Core Ops, SparseCore 0:
  548.0 15.8 all-gather.4
  731.6 24.0 all-gather.6
where the time goes:
time: 1150 us; the launch traced here: 1140 us
  waiting for transfers between devices  448 us (39%)
  matrix products  444 us (39%)
  local copies, waits for them, and re-layouts  183 us (16%)
  starting transfers between devices  50.6 us (4%)
  between operations  15.2 us (1%)
    all_to_all x1, waiting for transfers between devices, shards(): lax.all_to_all(value, 'head', split_axis=1, concat_axis=0, tiled=True)  88.1 us
    all_to_all x1, waiting for transfers between devices, shards(): lax.all_to_all(key, 'head', split_axis=1, concat_axis=0, tiled=True)  88.1 us
    all_to_all x1, waiting for transfers between devices, shards(): lax.all_to_all(grad_out, 'head', split_axis=1, concat_axis=0, tiled=True)  87.2 us
    dot_general x5, matrix products, finish(): jnp.einsum('ij,igde->jgde', mapping, products[level - 1], precision=lax.P...  86.3 us
    all_to_all x1, waiting for transfers between devices, shards(): lax.all_to_all(query, 'head', split_axis=1, concat_axis=0, tiled=True)  69 us
    dot_general x5, matrix products, finish(): jnp.einsum('ntge,ngde->ntgd', grad_blocks, read_state, preferred_element_...  65.6 us
    dot_general x5, matrix products, finish(): jnp.einsum('ij,jgde->igde', mapping, states, precision=lax.Precision.HIGH...  62.7 us
    convert_element_type x10, local copies, waits for them, and re-layouts, flatten(): return array.reshape(stretches * C, heads * width).astype(jnp.bfloat16)  57.8 us
  transfers between devices with their start and end apart: 12, of which 7 were waited for; matrix products, arithmetic and copies ran while one was open for 38% of the time, Pallas kernels for 0%

commit v1 on v0

--- a/solution.py
+++ b/solution.py
@@ -139,7 +139,12 @@
     query, key, value, grad_out, level_weights = (
         lax.all_to_all(query, "head", split_axis=1, concat_axis=0, tiled=True),
         lax.all_to_all(key, "head", split_axis=1, concat_axis=0, tiled=True),
-        lax.all_to_all(value, "head", split_axis=1, concat_axis=0, tiled=True),
+        jnp.concatenate(
+            lax.all_to_all(
+                jnp.stack(jnp.split(value, lax.axis_size("head"), axis=1)), "head", 0, 0
+            ),
+            axis=0,
+        ),
         lax.all_to_all(grad_out, "head", split_axis=1, concat_axis=0, tiled=True),
         lax.all_to_all(level_weights, "head", split_axis=1, concat_axis=0, tiled=True),
     )

time: 1150 us -> 1110 us (0.965)
  matrix products: 444 us -> 402 us
  local copies, waits for them, and re-layouts: 183 us -> 198 us
    all_to_all x1, waiting for transfers between devices: 88.1 us -> 51.7 us  [shards(): lax.all_to_all(jnp.stack(jnp.split(value, lax.axis_size('head'), axis=1))...]
    dot_general x5, matrix products: 65.6 us -> 42.6 us  [finish(): jnp.einsum('ntge,ngde->ntgd', grad_blocks, read_state, preferred_element_...]
    all_to_all x1, waiting for transfers between devices: 69 us -> 88.1 us  [shards(): lax.all_to_all(query, 'head', split_axis=1, concat_axis=0, tiled=True)]
    dot_general x5, matrix products: 62.7 us -> 44 us  [finish(): jnp.einsum('ij,jgde->igde', mapping, states, precision=lax.Precision.HIGH...]
    dot_general x7, matrix products: 46.9 us -> 31.1 us  [local_part(): jnp.einsum('ntgd,ntge->ngde', weighted, grad_blocks, preferred_element_ty...]
    dot_general x2, matrix products: 11 us -> 26.4 us  [finish(): jnp.einsum('ntge,gde->ntgd', grad_blocks, read_state, preferred_element_t...]
    unnamed x119 -> x125, local copies, waits for them, and re-layouts: 43.7 us -> 32.9 us
  transfers between devices with their start and end apart: 12 -> 12, of which waited for: 7 -> 8; matrix products, arithmetic and copies ran while one was open for 38% -> 41% of each run, Pallas kernels for 0% -> 0%
where the time goes in v1:
time: 1110 us
  waiting for transfers between devices  438 us (39%)
  matrix products  402 us (36%)
  local copies, waits for them, and re-layouts  198 us (18%)
  starting transfers between devices  49.7 us (4%)
  between operations  15.2 us (1%)
    all_to_all x1, waiting for transfers between devices, shards(): lax.all_to_all(query, 'head', split_axis=1, concat_axis=0, tiled=True)  88.1 us
    all_to_all x1, waiting for transfers between devices, shards(): lax.all_to_all(key, 'head', split_axis=1, concat_axis=0, tiled=True)  87.9 us
    all_to_all x1, waiting for transfers between devices, shards(): lax.all_to_all(grad_out, 'head', split_axis=1, concat_axis=0, tiled=True)  87.2 us
    dot_general x5, matrix products, finish(): jnp.einsum('ij,igde->jgde', mapping, products[level - 1], precision=lax.P...  86.1 us
    convert_element_type x10, local copies, waits for them, and re-layouts, flatten(): return array.reshape(stretches * C, heads * width).astype(jnp.bfloat16)  59 us
    all_to_all x1, waiting for transfers between devices, shards(): lax.all_to_all(results[2], 'head', split_axis=0, concat_axis=1, tiled=True)  56.3 us
    all_to_all x1, waiting for transfers between devices, shards(): lax.all_to_all(results[3], 'head', split_axis=0, concat_axis=1, tiled=True)  54 us
    all_to_all x1, waiting for transfers between devices, shards(): lax.all_to_all(jnp.stack(jnp.split(value, lax.axis_size('head'), axis=1))...  51.7 us
  transfers between devices with their start and end apart: 12, of which 8 were waited for; matrix products, arithmetic and copies ran while one was open for 41% of the time, Pallas kernels for 0%

profile of v1, /device:TPU:0, one launch (start us, length us, event | category | flops | bytes accessed | tf_op | source)
XLA Modules:
  0.0 1108.1 jit_solution(16490683352123702502)
XLA Ops:
  33.6 87.2 %all-to-all-done.5 = bf16[1024,4,512]{2,0,1:T(8,128)(2,1)} async-done(((bf16[1024,4,512]{2,0,1:T(8,128)(2,1)}), bf16[1024,4,512]{2,0,1:T(8,128)(2,1)}, u32[]{:S(2)}, u32[]{:S(2)}) %all-to-all-start.5) | async-done | bytes 4194336 | tf_op jit(solution)/shard_map/all_to_all | solution.py:148
  130.4 88.1 %all-to-all-done.2 = bf16[1024,4,512]{2,0,1:T(8,128)(2,1)} async-done(((bf16[1024,4,512]{2,0,1:T(8,128)(2,1)}), bf16[1024,4,512]{2,0,1:T(8,128)(2,1)}, u32[]{:S(2)}, u32[]{:S(2)}) %all-to-all-start.2) | async-done | bytes 4194336 | tf_op jit(solution)/shard_map/all_to_all | solution.py:140
  228.1 87.9 %all-to-all-done.3 = bf16[1024,4,512]{2,0,1:T(8,128)(2,1)} async-done(((bf16[1024,4,512]{2,0,1:T(8,128)(2,1)}), bf16[1024,4,512]{2,0,1:T(8,128)(2,1)}, u32[]{:S(2)}, u32[]{:S(2)}) %all-to-all-start.3) | async-done | bytes 4194336 | tf_op jit(solution)/shard_map/all_to_all | solution.py:141
  333.6 7.2 copy.340
  347.7 7.2 copy.316
  361.9 51.7 %all-to-all-done = bf16[4,1024,512]{2,1,0:T(8,128)(2,1)} async-done(((bf16[4,1024,512]{2,1,0:T(8,128)(2,1)}), bf16[4,1024,512]{2,1,0:T(8,128)(2,1)}, u32[]{:S(2)}, u32[]{:S(2)}) %all-to-all-start) | async-done | bytes 4194336 | tf_op jit(solution)/shard_map/all_to_all | solution.py:143
  420.4 8.5 fusion.243
  428.9 10.3 copy.260
  439.2 8.2 fusion.97
  447.4 8.6 multiply_convert_fusion.1
  456.0 8.0 fusion.70
  464.1 8.7 multiply_convert_fusion
  472.8 8.1 fusion.66
  480.9 7.7 fusion.68
  488.7 7.9 fusion.72
  496.6 8.2 multiply_convert_fusion.2
  504.7 8.1 fusion.74
  512.9 7.8 fusion.76
  520.6 8.7 multiply_convert_fusion.3
  529.3 8.1 fusion.78
  537.4 7.7 fusion.80
  546.1 9.9 multiply_convert_fusion.4
  558.0 8.2 fusion.82
  583.5 13.2 %fusion.35 = f32[32,4,128,128]{3,0,2,1:T(8,128)} fusion(f32[32,4,128,128]{3,2,1,0:T(8,128)S(1)} %fusion.49, s32[32]{0:T(128)S(1)} %fusion.209, s32[32]{0:T(128)S(1)} %and_select_fusion.7, pred[32]{0:T(512)(128)(4,1)S(1)} %fusion.208), kind=kOutput, calls=%fused_computation.67 | convolution fusion | flops 805309440 | bytes 16777504 | tf_op jit(solution)/shard_map/ij,igde->jgde/dot_general | solution.py:92
  600.9 7.2 fusion.120
  608.1 23.2 %fusion.13 = (bf16[32,128,4]{1,2,0:T(4,128)(2,1)S(1)}, bf16[32,128,4]{1,2,0:T(4,128)(2,1)S(1)}, bf16[32,128,4]{1,2,0:T(4,128)(2,1)S(1)}, bf16[32,128,4]{1,2,0:T(...) fusion(bf16[32,128,4,128]{1,3,2,0:T(8,128)(2,1)S(1)} %copy-done, ...), kind=kOutput, calls=%fused_computation.27 | convolution fusion | flops 568213504 | bytes 67469312 | tf_op jit(solution)/shard_map/ntgd,gde->ntge/dot_general | solution.py:98
  635.9 25.9 %fusion.28 = bf16[32,128,4,128]{1,3,2,0:T(8,128)(2,1)} fusion(f32[4,128,32,128]{3,1,0,2:T(8,128)} %get-tuple-element.49, f32[4,128,32,128]{3,1,0,2:T(8,128)} %fusion.120, f32[32,4,128,128]{3,2,1,0:T(8,128)} %fusion.66, f32[32,4,128,128]{3,2,1,0:T(8,128)} %fusion.70, f32[32,4,128,128]{3,2,1,0:T(8,128)} %fusion.74, f32[32,4,128,128]{3,2,1,0:T(8,128)} %fusion.78, ...), kind=kOutput, calls=%fused_computation.54 | convolution fusion | flops 574619648 | bytes 76087296 | tf_op jit(solution)/shard_map/ngts,nsgd->ntgd/dot_general | solution.py:42
  661.8 7.5 copy.293
  669.3 7.2 convert_element_type.131
  681.5 11.5 %fusion.84 = f32[32,4,128,128]{3,2,1,0:T(8,128)} fusion(bf16[32,128,4,128]{1,3,2,0:T(8,128)(2,1)} %copy.340, bf16[32,4,128,128]{3,0,2,1:T(8,128)(2,1)} %copy-done.13), kind=kOutput, calls=%fused_computation.120 | convolution fusion | flops 536870912 | bytes 16777216 | tf_op jit(solution)/shard_map/ntge,ngde->ntgd/dot_general | solution.py:89
  696.1 13.2 %fusion.37 = f32[32,4,128,128]{3,0,2,1:T(8,128)} fusion(f32[32,4,128,128]{3,2,1,0:T(8,128)S(1)} %fusion.51, s32[32]{0:T(128)S(1)} %copy-done.47, s32[32]{0:T(128)S(1)} %copy-done.49, pred[32]{0:T(512)(128)(4,1)S(1)} %copy-done.51), kind=kOutput, calls=%fused_computation.69 | convolution fusion | flops 805309440 | bytes 16777504 | tf_op jit(solution)/shard_map/ij,igde->jgde/dot_general | solution.py:92
  715.6 8.6 fusion.94
  728.8 21.9 %fusion.17 = bf16[32,128,4,128]{1,3,2,0:T(8,128)(2,1)} fusion(f32[4,128,32,128]{3,1,0,2:T(8,128)} %fusion.118, f32[32,4,128,128]{3,2,1,0:T(8,128)} %fusion.68, f32[32,4,128,128]{3,2,1,0:T(8,128)} %fusion.72, f32[32,4,128,128]{3,2,1,0:T(8,128)} %fusion.76, f32[32,4,128,128]{3,2,1,0:T(8,128)} %fusion.80, f32[32,4,128,128]{3,2,1,0:T(8,128)} %fusion.84, ...), kind=kOutput, calls=%fused_computation.34 | convolution fusion | flops 568328192 | bytes 67698688 | tf_op jit(solution)/shard_map/ntge,gde->ntgd/dot_general | solution.py:101
  750.6 7.8 copy.313
  758.4 7.2 convert_element_type.134
  765.7 8.1 all-to-all-done.4
  778.7 17.3 %fusion.39 = f32[32,4,128,128]{3,0,2,1:T(8,128)} fusion(f32[32,4,128,128]{3,2,1,0:T(8,128)} %fusion.53, s32[32]{0:T(128)S(1)} %copy-done.41, s32[32]{0:T(128)S(1)} %copy-done.43, pred[32]{0:T(512)(128)(4,1)S(1)} %copy-done.45), kind=kOutput, calls=%fused_computation.71 | convolution fusion | flops 805309440 | bytes 16777504 | tf_op jit(solution)/shard_map/ij,igde->jgde/dot_general | solution.py:92
  802.4 17.4 %fusion.41 = f32[32,4,128,128]{3,0,2,1:T(8,128)} fusion(f32[32,4,128,128]{3,2,1,0:T(8,128)} %fusion.55, s32[32]{0:T(128)S(1)} %copy-done.35, s32[32]{0:T(128)S(1)} %copy-done.37, pred[32]{0:T(512)(128)(4,1)S(1)} %copy-done.39), kind=kOutput, calls=%fused_computation.73 | convolution fusion | flops 805309440 | bytes 16777504 | tf_op jit(solution)/shard_map/ij,igde->jgde/dot_general | solution.py:92
  840.0 25.1 %add_convert_fusion = bf16[32,4,128,128]{3,0,2,1:T(8,128)(2,1)} fusion(f32[32,4,128,128]{3,0,2,1:T(8,128)} %fusion.35, f32[32,4,128,128]{3,0,2,1:T(8,128)} %fusion.37, f32[32,4,128,128]{3,0,2,1:T(8,128)} %fusion.39, f32[32,4,128,128]{3,0,2,1:T(8,128)} %fusion.41, f32[4,128,128]{2,1,0:T(8,128)S(1)} %bitcast.328, f32[4,128,128]{2,1,0:T(8,128)S(1)} %bitcast.327, ...), kind=kOutput, calls=%fused_computation.77 | convolution fusion | flops 830475264 | bytes 46661792 | tf_op jit(solution)/shard_map/ij,igde->jgde/dot_general | solution.py:92
  865.1 7.5 copy.335
  872.6 7.1 fusion.15
  885.7 7.2 convert_element_type.145
  898.3 11.0 fusion.109
  909.3 9.8 fusion.14
  919.1 8.2 copy.338
  927.3 7.2 convert_element_type.147
  934.5 56.3 %all-to-all-done.7 = bf16[4,1024,512]{2,1,0:T(8,128)(2,1)} async-done(((bf16[4,1024,512]{2,1,0:T(8,128)(2,1)}), bf16[4,1024,512]{2,1,0:T(8,128)(2,1)}, u32[]{:S(2)}, u32[]{:S(2)}) %all-to-all-start.7) | async-done | bytes 4194336 | tf_op jit(solution)/shard_map/all_to_all | solution.py:175
  1034.4 54.0 %all-to-all-done.8 = bf16[4,1024,512]{2,1,0:T(8,128)(2,1)} async-done(((bf16[4,1024,512]{2,1,0:T(8,128)(2,1)}), bf16[4,1024,512]{2,1,0:T(8,128)(2,1)}, u32[]{:S(2)}, u32[]{:S(2)}) %all-to-all-start.8) | async-done | bytes 4194336 | tf_op jit(solution)/shard_map/all_to_all | solution.py:176
  (213 shorter events, 230.6 us)
Async XLA Ops:
  9.0 15.2 %all-to-all-start.1 = ((bf16[1024,4,32]{0,2,1:T(8,128)(2,1)}), bf16[1024,4,32]{0,2,1:T(8,128)(2,1)S(1)}, u32[]{:S(2)}, u32[]{:S(2)}) async-start(bf16[1024,4,32]{0,2,1:T(8,128)(2,1)} %bitcast.4), calls=%async_computation.1 | async-start | bytes 524288 | tf_op jit(solution)/shard_map/all_to_all | solution.py:149
  24.2 96.7 %all-to-all-start.5 = ((bf16[1024,4,512]{2,0,1:T(8,128)(2,1)}), bf16[1024,4,512]{2,0,1:T(8,128)(2,1)}, u32[]{:S(2)}, u32[]{:S(2)}) async-start(bf16[1024,4,512]{2,0,1:T(8,128)(2,1)} %bitcast.316), calls=%async_computation.5 | async-start | bytes 8388608 | tf_op jit(solution)/shard_map/all_to_all | solution.py:148
  120.9 97.6 %all-to-all-start.2 = ((bf16[1024,4,512]{2,0,1:T(8,128)(2,1)}), bf16[1024,4,512]{2,0,1:T(8,128)(2,1)}, u32[]{:S(2)}, u32[]{:S(2)}) async-start(bf16[1024,4,512]{2,0,1:T(8,128)(2,1)} %bitcast.317), calls=%async_computation.2 | async-start | bytes 8388608 | tf_op jit(solution)/shard_map/all_to_all | solution.py:140
  218.5 97.5 %all-to-all-start.3 = ((bf16[1024,4,512]{2,0,1:T(8,128)(2,1)}), bf16[1024,4,512]{2,0,1:T(8,128)(2,1)}, u32[]{:S(2)}, u32[]{:S(2)}) async-start(bf16[1024,4,512]{2,0,1:T(8,128)(2,1)} %bitcast.315), calls=%async_computation.3 | async-start | bytes 8388608 | tf_op jit(solution)/shard_map/all_to_all | solution.py:141
  316.0 97.6 %all-to-all-start = ((bf16[4,1024,512]{2,1,0:T(8,128)(2,1)}), bf16[4,1024,512]{2,1,0:T(8,128)(2,1)}, u32[]{:S(2)}, u32[]{:S(2)}) async-start(bf16[4,1024,512]{2,1,0:T(8,128)(2,1)} %pad_maximum_fusion), calls=%async_computation | async-start | bytes 8388608 | tf_op jit(solution)/shard_map/all_to_all | solution.py:143
  320.9 275.9 %all-gather.5.cloned.1.call-start = ((), (), s32[]{:S(2)}) async-start(), calls=%async_computation.10 | async-start | bytes 1310720 | tf_op jit(solution)/shard_map/all_gather | solution.py:158
  321.2 199.5 %copy-start.34 = (s32[32]{0:T(128)}, s32[32]{0:T(128)S(1)}, u32[]{:S(2)}) copy-start(s32[32]{0:T(128)S(1)} %broadcast_multiply_fusion.2) | copy-start | bytes 388
  321.2 199.4 %copy-start.36 = (s32[32]{0:T(128)}, s32[32]{0:T(128)S(1)}, u32[]{:S(2)}) copy-start(s32[32]{0:T(128)S(1)} %and_select_fusion.13) | copy-start | bytes 388
  321.2 199.4 %copy-start.38 = (pred[32]{0:T(512)(128)(4,1)}, pred[32]{0:T(512)(128)(4,1)S(1)}, u32[]{:S(2)}) copy-start(pred[32]{0:T(512)(128)(4,1)S(1)} %fusion.205) | copy-start | bytes 100
  321.3 175.3 %copy-start.40 = (s32[32]{0:T(128)}, s32[32]{0:T(128)S(1)}, u32[]{:S(2)}) copy-start(s32[32]{0:T(128)S(1)} %broadcast_multiply_fusion.1) | copy-start | bytes 388
  321.3 175.3 %copy-start.42 = (s32[32]{0:T(128)}, s32[32]{0:T(128)S(1)}, u32[]{:S(2)}) copy-start(s32[32]{0:T(128)S(1)} %and_select_fusion.11) | copy-start | bytes 388
  321.3 175.3 %copy-start.44 = (pred[32]{0:T(512)(128)(4,1)}, pred[32]{0:T(512)(128)(4,1)S(1)}, u32[]{:S(2)}) copy-start(pred[32]{0:T(512)(128)(4,1)S(1)} %fusion.206) | copy-start | bytes 100
  321.3 126.1 %copy-start.46 = (s32[32]{0:T(128)}, s32[32]{0:T(128)S(1)}, u32[]{:S(2)}) copy-start(s32[32]{0:T(128)S(1)} %broadcast_multiply_fusion) | copy-start | bytes 388
  321.3 126.1 %copy-start.48 = (s32[32]{0:T(128)}, s32[32]{0:T(128)S(1)}, u32[]{:S(2)}) copy-start(s32[32]{0:T(128)S(1)} %and_select_fusion.9) | copy-start | bytes 388
  321.4 126.0 %copy-start.50 = (pred[32]{0:T(512)(128)(4,1)}, pred[32]{0:T(512)(128)(4,1)S(1)}, u32[]{:S(2)}) copy-start(pred[32]{0:T(512)(128)(4,1)S(1)} %fusion.207) | copy-start | bytes 100
  321.4 224.6 %copy-start.30 = (s32[32]{0:T(128)}, s32[32]{0:T(128)S(1)}, u32[]{:S(2)}) copy-start(s32[32]{0:T(128)S(1)} %broadcast_multiply_fusion.3) | copy-start | bytes 388
  321.4 224.6 %copy-start.32 = (pred[32]{0:T(512)(128)(4,1)}, pred[32]{0:T(512)(128)(4,1)S(1)}, u32[]{:S(2)}) copy-start(pred[32]{0:T(512)(128)(4,1)S(1)} %fusion.204) | copy-start | bytes 100
  323.3 242.8 %copy-start.25 = (f32[32,128,4]{1,2,0:T(4,128)}, f32[32,128,4]{1,2,0:T(4,128)S(1)}, u32[]{:S(2)}) copy-start(f32[32,128,4]{1,2,0:T(4,128)S(1)} %copy.289) | copy-start | bytes 196612
  323.4 244.1 %copy-start.27 = (f32[32,128,4]{1,2,0:T(4,128)}, f32[32,128,4]{1,2,0:T(4,128)S(1)}, u32[]{:S(2)}) copy-start(f32[32,128,4]{1,2,0:T(4,128)S(1)} %copy.283) | copy-start | bytes 196612
  323.4 253.6 %copy-start.19 = (f32[32,128,4]{1,2,0:T(4,128)}, f32[32,128,4]{1,2,0:T(4,128)S(1)}, u32[]{:S(2)}) copy-start(f32[32,128,4]{1,2,0:T(4,128)S(1)} %copy.278) | copy-start | bytes 196612
  546.0 286.5 %all-gather.7.cloned.1.call-start = ((), (), s32[]{:S(2)}) async-start(), calls=%async_computation.11 | async-start | bytes 2621440 | tf_op jit(solution)/shard_map/all_gather | solution.py:159
  546.1 11.9 %copy-start.6 = (bf16[32,128,4,128]{1,3,2,0:T(8,128)(2,1)S(1)}, bf16[32,128,4,128]{1,3,2,0:T(8,128)(2,1)}, u32[]{:S(2)}) copy-start(bf16[32,128,4,128]{1,3,2,0:T(8,128)(2,1)} %copy.316) | copy-start | bytes 12582916
  608.1 27.8 %copy-start.14 = (f32[32,4,128]{2,1,0:T(4,128)S(1)}, f32[32,4,128]{2,1,0:T(4,128)}, u32[]{:S(2)}) copy-start(f32[32,4,128]{2,1,0:T(4,128)} %copy.249) | copy-start | bytes 196612
  608.1 27.8 %copy-start.15 = (f32[32,128,4]{1,2,0:T(4,128)S(1)}, f32[32,128,4]{1,2,0:T(4,128)}, u32[]{:S(2)}) copy-start(f32[32,128,4]{1,2,0:T(4,128)} %copy.256) | copy-start | bytes 196612
  608.1 27.8 %copy-start.17 = (f32[32,128,4]{1,2,0:T(4,128)S(1)}, f32[32,128,4]{1,2,0:T(4,128)}, u32[]{:S(2)}) copy-start(f32[32,128,4]{1,2,0:T(4,128)} %copy.263) | copy-start | bytes 196612
  608.1 27.8 %copy-start.20 = (f32[32,128,4]{1,2,0:T(4,128)S(1)}, f32[32,128,4]{1,2,0:T(4,128)}, u32[]{:S(2)}) copy-start(f32[32,128,4]{1,2,0:T(4,128)} %copy-done.19) | copy-start | bytes 196612
  608.1 27.8 %copy-start.21 = (f32[32,128,4]{1,2,0:T(4,128)S(1)}, f32[32,128,4]{1,2,0:T(4,128)}, u32[]{:S(2)}) copy-start(f32[32,128,4]{1,2,0:T(4,128)} %copy.273) | copy-start | bytes 196612
  608.1 27.8 %copy-start.23 = (f32[32,128,4]{1,2,0:T(4,128)S(1)}, f32[32,128,4]{1,2,0:T(4,128)}, u32[]{:S(2)}) copy-start(f32[32,128,4]{1,2,0:T(4,128)} %copy.268) | copy-start | bytes 196612
  608.1 27.8 %copy-start.26 = (f32[32,128,4]{1,2,0:T(4,128)S(1)}, f32[32,128,4]{1,2,0:T(4,128)}, u32[]{:S(2)}) copy-start(f32[32,128,4]{1,2,0:T(4,128)} %copy-done.25) | copy-start | bytes 196612
  608.1 27.8 %copy-start.28 = (f32[32,128,4]{1,2,0:T(4,128)S(1)}, f32[32,128,4]{1,2,0:T(4,128)}, u32[]{:S(2)}) copy-start(f32[32,128,4]{1,2,0:T(4,128)} %copy-done.27) | copy-start | bytes 196612
  632.4 44.0 %all-to-all-start.9 = ((bf16[4,1024,32]{1,2,0:T(8,128)(2,1)}), bf16[4,1024,32]{1,2,0:T(8,128)(2,1)S(1)}, u32[]{:S(2)}, u32[]{:S(2)}) async-start(bf16[4,1024,32]{1,2,0:T(8,128)(2,1)} %copy.342), calls=%async_computation.9 | async-start | bytes 524288 | tf_op jit(solution)/shard_map/all_to_all | solution.py:177
  676.4 97.3 %all-to-all-start.4 = ((bf16[4,1024,512]{2,1,0:T(8,128)(2,1)}), bf16[4,1024,512]{2,1,0:T(8,128)(2,1)}, u32[]{:S(2)}, u32[]{:S(2)}) async-start(bf16[4,1024,512]{2,1,0:T(8,128)(2,1)} %convert_element_type.131), calls=%async_computation.4 | async-start | bytes 8388608 | tf_op jit(solution)/shard_map/all_to_all | solution.py:173
  681.5 11.5 %copy-start.3 = (bf16[32,128,4,128]{1,3,2,0:T(8,128)(2,1)S(1)}, bf16[32,128,4,128]{1,3,2,0:T(8,128)(2,1)}, u32[]{:S(2)}) copy-start(bf16[32,128,4,128]{1,3,2,0:T(8,128)(2,1)} %copy.340) | copy-start | bytes 12582916
  681.5 11.5 %copy-start.7 = (bf16[32,128,4,128]{1,3,2,0:T(8,128)(2,1)S(1)}, bf16[32,128,4,128]{1,3,2,0:T(8,128)(2,1)}, u32[]{:S(2)}) copy-start(bf16[32,128,4,128]{1,3,2,0:T(8,128)(2,1)} %copy.316) | copy-start | bytes 12582916
  681.5 11.5 %copy-start.22 = (f32[32,128,4]{1,2,0:T(4,128)S(1)}, f32[32,128,4]{1,2,0:T(4,128)}, u32[]{:S(2)}) copy-start(f32[32,128,4]{1,2,0:T(4,128)} %copy.273) | copy-start | bytes 196612
  696.1 13.2 %copy-start.24 = (f32[32,128,4]{1,2,0:T(4,128)S(1)}, f32[32,128,4]{1,2,0:T(4,128)}, u32[]{:S(2)}) copy-start(f32[32,128,4]{1,2,0:T(4,128)} %copy.268) | copy-start | bytes 196612
  765.6 13.0 %copy-start.41 = (s32[32]{0:T(128)S(1)}, s32[32]{0:T(128)}, u32[]{:S(2)}) copy-start(s32[32]{0:T(128)} %copy-done.40) | copy-start | bytes 388
  765.6 13.0 %copy-start.43 = (s32[32]{0:T(128)S(1)}, s32[32]{0:T(128)}, u32[]{:S(2)}) copy-start(s32[32]{0:T(128)} %copy-done.42) | copy-start | bytes 388
  765.7 13.0 %copy-start.45 = (pred[32]{0:T(512)(128)(4,1)S(1)}, pred[32]{0:T(512)(128)(4,1)}, u32[]{:S(2)}) copy-start(pred[32]{0:T(512)(128)(4,1)} %copy-done.44) | copy-start | bytes 100
  773.7 119.1 %all-to-all-start.6 = ((bf16[4,1024,512]{2,1,0:T(8,128)(2,1)}), bf16[4,1024,512]{2,1,0:T(8,128)(2,1)}, u32[]{:S(2)}, u32[]{:S(2)}) async-start(bf16[4,1024,512]{2,1,0:T(8,128)(2,1)} %convert_element_type.134), calls=%async_computation.6 | async-start | bytes 8388608 | tf_op jit(solution)/shard_map/all_to_all | solution.py:174
  778.7 17.3 %copy-start.4 = (bf16[32,128,4,128]{1,3,2,0:T(8,128)(2,1)S(1)}, bf16[32,128,4,128]{1,3,2,0:T(8,128)(2,1)}, u32[]{:S(2)}) copy-start(bf16[32,128,4,128]{1,3,2,0:T(8,128)(2,1)} %copy.340) | copy-start | bytes 12582916
  778.7 17.3 %copy-start.8 = (bf16[32,128,4,128]{1,3,2,0:T(8,128)(2,1)S(1)}, bf16[32,128,4,128]{1,3,2,0:T(8,128)(2,1)}, u32[]{:S(2)}) copy-start(bf16[32,128,4,128]{1,3,2,0:T(8,128)(2,1)} %copy.316) | copy-start | bytes 12582916
  778.7 17.3 %copy-start.18 = (f32[32,128,4]{1,2,0:T(4,128)S(1)}, f32[32,128,4]{1,2,0:T(4,128)}, u32[]{:S(2)}) copy-start(f32[32,128,4]{1,2,0:T(4,128)} %copy.263) | copy-start | bytes 196612
  802.3 17.4 %copy-start.16 = (f32[32,128,4]{1,2,0:T(4,128)S(1)}, f32[32,128,4]{1,2,0:T(4,128)}, u32[]{:S(2)}) copy-start(f32[32,128,4]{1,2,0:T(4,128)} %copy.256) | copy-start | bytes 196612
  802.4 23.7 %slice-start.2 = ((s8[8388608]{0:T(1024)(128)(4,1)}), s8[4194304]{0:T(1024)(128)(4,1)S(1)}, s32[]{:S(2)}) async-start(s8[8388608]{0:T(1024)(128)(4,1)} %bitcast.313), calls=%async_computation.14 | async-start | bytes 8388608
  892.8 98.0 %all-to-all-start.7 = ((bf16[4,1024,512]{2,1,0:T(8,128)(2,1)}), bf16[4,1024,512]{2,1,0:T(8,128)(2,1)}, u32[]{:S(2)}, u32[]{:S(2)}) async-start(bf16[4,1024,512]{2,1,0:T(8,128)(2,1)} %convert_element_type.145), calls=%async_computation.7 | async-start | bytes 8388608 | tf_op jit(solution)/shard_map/all_to_all | solution.py:175
  898.3 11.1 copy-start.11
  990.8 97.6 %all-to-all-start.8 = ((bf16[4,1024,512]{2,1,0:T(8,128)(2,1)}), bf16[4,1024,512]{2,1,0:T(8,128)(2,1)}, u32[]{:S(2)}, u32[]{:S(2)}) async-start(bf16[4,1024,512]{2,1,0:T(8,128)(2,1)} %convert_element_type.147), calls=%async_computation.8 | async-start | bytes 8388608 | tf_op jit(solution)/shard_map/all_to_all | solution.py:176
  (20 other events, 113.3 us)
Sparse Core Ops, SparseCore 0:
  546.1 15.8 all-gather.4
  596.8 21.6 all-gather.6
